TPU v7x, 32 devices: a whole 2x2x4 slice. The times are simulated.
32 devices in a mesh: layer: 2 (over core), row: 4 (over z), rep: 4 (over y, x).
Axes of the slice: x: 2, y: 2, z: 4, core: 2. Of those that a mesh axis runs over, the one named last changes fastest.
Arguments:
- features: bfloat16 [2048, 256], P(('row', 'rep')), may hold values from -6 to 6
- class_ids: int32 [2048], P(('row', 'rep')), may hold values from 0 to 256
- label_table: bfloat16 [256, 256], replicated, may hold values from -3 to 3
- self_weight: bfloat16 [2, 256, 256], P('layer'), may hold values from -0.375 to 0.375
- neighbor_weight: bfloat16 [2, 256, 256], P('layer'), may hold values from -0.375 to 0.375
- norm_scale: float32 [256], replicated, may hold values from 0.1 to 1.9
- tile_values: bfloat16 [4, 4, 32, 128, 128], P('row', 'rep')
- tile_block_row: int32 [4, 4, 32], P('row', 'rep'), may hold values from 0 to 3, as said below
- tile_section: int32 [4, 4, 32], P('row', 'rep'), may hold values from 0 to 3
- tile_count: int32 [4, 4], P('row', 'rep'), may hold values from 4 to 32, as said below
Outputs:
- hidden_states: bfloat16 [2, 2048, 256], P('layer', ('row', 'rep'))
Inputs may be any that keep to these rules, and one draw needn't show every extreme that they name: `class_ids`: 256 marks a node without a label. `tile_block_row`: slots 0 to 3 of every device name block rows 0 to 3 in order. `tile_count`: at least 4; 32 on some device.
All inputs are finite; a program needn't handle non-finite values.
Results may differ from a plain program's by a relative error of at most 0.0052.
Values may be sent and summed in bfloat16 or wider, within the bound.
No kernel may reach another device: no remote copies, remote signals or barrier semaphores. Data moves between devices by JAX's collectives and lax.ppermute only.
A program may use at most 64 MiB of HBM per device.

v0:
```python
import jax
import jax.numpy as jnp
from jax import lax
from jax.sharding import PartitionSpec as P


def shifted(value, axis, steps):
    count = lax.axis_size(axis)
    leading, last = (max(0, -steps), min(count, count - steps))
    return lax.ppermute(value, axis, [(source, source + steps) for source in range(leading, last)])


def settle(mixture, norm_scale, first):
    if first:
        active = jnp.maximum(mixture, 0.0)
        center = active - jnp.mean(active, axis=-1, keepdims=True)
        spread = jnp.mean(center * center, axis=-1, keepdims=True)
        return (center * lax.rsqrt(spread + 1e-05) * norm_scale).astype(jnp.bfloat16)
    return mixture.astype(jnp.bfloat16)


def body(
    features,
    class_ids,
    label_table,
    self_weight,
    neighbor_weight,
    norm_scale,
    tile_values,
    tile_block_row,
    tile_section,
    tile_count,
):
    which_layer = lax.axis_index("layer")
    groups = lax.axis_size("row")
    splits = lax.axis_size("rep")
    tile_data = tile_values[0, 0]
    block_rows = tile_block_row[0, 0]
    sections = tile_section[0, 0]
    filled = tile_count[0, 0]
    slot_total = tile_data.shape[0]
    tile_edge = tile_data.shape[1]
    hidden_dim = features.shape[1]
    classes = label_table.shape[0]
    one_hot = (class_ids[:, None] == jnp.arange(classes, dtype=jnp.int32)[None, :]).astype(
        jnp.bfloat16
    )
    inputs = (
        features.astype(jnp.float32)
        + jnp.dot(one_hot, label_table, preferred_element_type=jnp.float32)
    ).astype(jnp.bfloat16)
    slot_ids = jnp.arange(slot_total, dtype=jnp.int32)
    targets = jnp.arange(splits, dtype=jnp.int32)

    def placement(keep_mask):
        live = jnp.logical_and(slot_ids < filled, keep_mask)
        return jnp.logical_and(block_rows[None, :] == targets[:, None], live[None, :]).astype(
            jnp.float32
        )

    outcomes = []
    all_slots = slot_ids >= 0
    tile_sums = jnp.sum(tile_data, axis=-1, dtype=jnp.float32)
    row_sums = jnp.dot(placement(all_slots), tile_sums, precision=lax.Precision.HIGHEST).reshape(
        splits * tile_edge
    )
    current = inputs
    for layer_no in range(2):
        gathered = lax.all_gather(current, "row", axis=0, tiled=True)
        panel_rows = gathered.reshape(groups, tile_edge, hidden_dim)
        weights_on = placement(all_slots)

        def add_tiles(batch_no, running):
            offset = batch_no * 8
            tile_batch = lax.dynamic_slice_in_dim(tile_data, offset, 8, 0)
            where_from = lax.dynamic_slice_in_dim(sections, offset, 8, 0)
            onto_rows = lax.dynamic_slice_in_dim(weights_on, offset, 8, 1)
            sources = panel_rows[where_from]
            products = jnp.einsum(
                "kab,kbf->kaf", tile_batch, sources, preferred_element_type=jnp.float32
            )
            return running + jnp.einsum(
                "sk,kaf->saf", onto_rows, products, precision=lax.Precision.HIGHEST
            )

        running = jnp.zeros((splits, tile_edge, hidden_dim), jnp.float32)
        running = lax.fori_loop(0, slot_total // 8, add_tiles, running)
        partial_value = running.reshape(splits * tile_edge, hidden_dim)
        if layer_no == 0:
            summed, degree = (
                lax.psum_scatter(partial_value, "rep", scatter_dimension=0, tiled=True),
                lax.psum_scatter(row_sums, "rep", scatter_dimension=0, tiled=True),
            )
        else:
            summed = lax.psum_scatter(partial_value, "rep", scatter_dimension=0, tiled=True)
        neighbor = (summed * lax.rsqrt(degree)[:, None]).astype(jnp.bfloat16)
        mixture = jnp.dot(current, self_weight[0], preferred_element_type=jnp.float32) + jnp.dot(
            neighbor, neighbor_weight[0], preferred_element_type=jnp.float32
        )
        result = jnp.where(
            which_layer == 0, settle(mixture, norm_scale, True), settle(mixture, norm_scale, False)
        )
        outcomes.append(result)
        if layer_no == 0:
            current = shifted(result, "layer", 1)
    selected = jnp.where(which_layer == 0, outcomes[0], outcomes[1])
    return selected[None]


def solution(mesh):
    return jax.shard_map(
        body,
        mesh=mesh,
        in_specs=(
            P(("row", "rep"), None),
            P(("row", "rep")),
            P(),
            P("layer", None, None),
            P("layer", None, None),
            P(),
            P("row", "rep", None, None, None),
            P("row", "rep", None),
            P("row", "rep", None),
            P("row", "rep"),
        ),
        out_specs=P("layer", ("row", "rep"), None),
        check_vma=False,
    )
```

profile of v0, /device:TPU:0, one launch (start us, length us, event | category | flops | bytes accessed | tf_op | source)
XLA Modules:
  0.0 137.9 jit_solution(1256336047873248968)
XLA Ops:
  7.2 1.1 fusion.14
  8.4 15.7 %all_gather.6 = bf16[512,256]{1,0:T(8,128)(2,1)S(1)} all-gather(bf16[128,256]{1,0:T(8,128)(2,1)S(1)} %fusion.14), channel_id=1, replica_groups=mesh['layer'=2,'row'=4,'rep'=4] {'row'}, dimensions={0}, use_global_device_ids=true | all-gather | bytes 327680 | tf_op jit(solution)/shard_map/all_gather | solution.py:69
  24.7 17.7 %while.28 = (s32[]{:T(128)}, f32[4,128,256]{2,0,1:T(4,128)S(1)}, f32[4,32]{1,0:T(4,128)S(1)}, bf16[32,128,128]{2,1,0:T(8,128)(2,1)}, s32[32]{0:T(128)}, /*index=...) while((s32[]{:T(128)}, f32[4,128,256]{2,0,1:T(4,128)S(1)}, ...), condition=%wide.region_1.0_spmd.clone, body=%wide.region_0.0_spmd.clone.sunk | while | flops 79954976 | bytes 4985641 | solution.py:87
  26.0 1.2 fusion.53
  27.3 1.8 %convolution_add_fusion.7 = f32[4,128,256]{2,0,1:T(4,128)S(1)} fusion(f32[8,128,256]{2,1,0:T(8,128)S(1)} %fusion.53, f32[4,128,256]{2,0,1:T(4,128)S(1)} %get-tuple-element.380, pred[]{:T(512)S(6)} %compare.6, f32[4,32]{1,0:T(4,128)S(1)} %get-tuple-element.391, s32[]{:T(128)S(6)} %select_n.78), kind=kOutput, calls=%fused_computation.2.clone.1 | convolution fusion | flops 12845056 | bytes 2097669 | tf_op jit(solution)/shard_map/while/body/eval_jaxpr/sk,kaf->saf/dot_general | solution.py:82
  30.5 1.2 fusion.53
  31.7 1.8 %convolution_add_fusion.7 = f32[4,128,256]{2,0,1:T(4,128)S(1)} fusion(f32[8,128,256]{2,1,0:T(8,128)S(1)} %fusion.53, f32[4,128,256]{2,0,1:T(4,128)S(1)} %get-tuple-element.380, pred[]{:T(512)S(6)} %compare.6, f32[4,32]{1,0:T(4,128)S(1)} %get-tuple-element.391, s32[]{:T(128)S(6)} %select_n.78), kind=kOutput, calls=%fused_computation.2.clone.1 | convolution fusion | flops 12845056 | bytes 2097669 | tf_op jit(solution)/shard_map/while/body/eval_jaxpr/sk,kaf->saf/dot_general | solution.py:82
  34.9 1.2 fusion.53
  36.2 1.8 %convolution_add_fusion.7 = f32[4,128,256]{2,0,1:T(4,128)S(1)} fusion(f32[8,128,256]{2,1,0:T(8,128)S(1)} %fusion.53, f32[4,128,256]{2,0,1:T(4,128)S(1)} %get-tuple-element.380, pred[]{:T(512)S(6)} %compare.6, f32[4,32]{1,0:T(4,128)S(1)} %get-tuple-element.391, s32[]{:T(128)S(6)} %select_n.78), kind=kOutput, calls=%fused_computation.2.clone.1 | convolution fusion | flops 12845056 | bytes 2097669 | tf_op jit(solution)/shard_map/while/body/eval_jaxpr/sk,kaf->saf/dot_general | solution.py:82
  39.3 1.2 fusion.53
  40.6 1.8 %convolution_add_fusion.7 = f32[4,128,256]{2,0,1:T(4,128)S(1)} fusion(f32[8,128,256]{2,1,0:T(8,128)S(1)} %fusion.53, f32[4,128,256]{2,0,1:T(4,128)S(1)} %get-tuple-element.380, pred[]{:T(512)S(6)} %compare.6, f32[4,32]{1,0:T(4,128)S(1)} %get-tuple-element.391, s32[]{:T(128)S(6)} %select_n.78), kind=kOutput, calls=%fused_computation.2.clone.1 | convolution fusion | flops 12845056 | bytes 2097669 | tf_op jit(solution)/shard_map/while/body/eval_jaxpr/sk,kaf->saf/dot_general | solution.py:82
  42.5 0.9 copy.15
  45.1 9.9 %all-reduce = f32[512]{0:T(512)S(1)} all-reduce(f32[512]{0:T(512)S(1)} %convolution_bitcast_fusion), channel_id=3, replica_groups=mesh['layer'=2,'row'=4,'rep'=4] {'rep'}, use_global_device_ids=true, to_apply=%region_4.0.clone | all-reduce | flops 512 | bytes 4096
  55.3 14.9 %reduce-scatter.3.cloned.1.call-done = f32[128,256]{1,0:T(8,128)} async-done(((f32[512,256]{1,0:T(8,128)}), f32[128,256]{1,0:T(8,128)}) %reduce-scatter.3.cloned.1.call-update) | async-done | bytes 131088 | tf_op jit(solution)/shard_map/reduce_scatter | solution.py:91
  70.2 1.2 maximum_reduce_fusion.1
  71.7 1.4 collective-permute-start
  74.0 14.0 %all_gather.7 = bf16[512,256]{1,0:T(8,128)(2,1)S(1)} all-gather(bf16[128,256]{1,0:T(8,128)(2,1)S(1)} %collective-permute-done), channel_id=1, replica_groups=mesh['layer'=2,'row'=4,'rep'=4] {'row'}, dimensions={0}, use_global_device_ids=true | all-gather | bytes 327680 | tf_op jit(solution)/shard_map/all_gather | solution.py:69
  88.0 13.9 %while.29 = (s32[]{:T(128)}, f32[4,128,256]{2,0,1:T(4,128)S(1)}, f32[4,32]{1,0:T(4,128)S(1)}, bf16[32,128,128]{2,1,0:T(8,128)(2,1)S(1)}, s32[32]{0:T(128)}, /*in...) while((s32[]{:T(128)}, f32[4,128,256]{2,0,1:T(4,128)S(1)}, ...), condition=%wide.region_8.9_spmd.clone, body=%wide.region_7.8_spmd.clone.sunk | while | flops 79954976 | bytes 4985641 | solution.py:87
  89.6 1.8 %convolution_add_fusion.8 = f32[4,128,256]{2,0,1:T(4,128)S(1)} fusion(f32[8,128,256]{2,1,0:T(8,128)S(1)} %fusion.58, f32[4,128,256]{2,0,1:T(4,128)S(1)} %get-tuple-element.410, pred[]{:T(512)S(6)} %compare.7, f32[4,32]{1,0:T(4,128)S(1)} %get-tuple-element.421, s32[]{:T(128)S(6)} %select_n.80), kind=kOutput, calls=%fused_computation.12.clone.1 | convolution fusion | flops 12845056 | bytes 2097669 | tf_op jit(solution)/shard_map/while/body/eval_jaxpr/sk,kaf->saf/dot_general | solution.py:82
  93.1 1.8 %convolution_add_fusion.8 = f32[4,128,256]{2,0,1:T(4,128)S(1)} fusion(f32[8,128,256]{2,1,0:T(8,128)S(1)} %fusion.58, f32[4,128,256]{2,0,1:T(4,128)S(1)} %get-tuple-element.410, pred[]{:T(512)S(6)} %compare.7, f32[4,32]{1,0:T(4,128)S(1)} %get-tuple-element.421, s32[]{:T(128)S(6)} %select_n.80), kind=kOutput, calls=%fused_computation.12.clone.1 | convolution fusion | flops 12845056 | bytes 2097669 | tf_op jit(solution)/shard_map/while/body/eval_jaxpr/sk,kaf->saf/dot_general | solution.py:82
  96.6 1.8 %convolution_add_fusion.8 = f32[4,128,256]{2,0,1:T(4,128)S(1)} fusion(f32[8,128,256]{2,1,0:T(8,128)S(1)} %fusion.58, f32[4,128,256]{2,0,1:T(4,128)S(1)} %get-tuple-element.410, pred[]{:T(512)S(6)} %compare.7, f32[4,32]{1,0:T(4,128)S(1)} %get-tuple-element.421, s32[]{:T(128)S(6)} %select_n.80), kind=kOutput, calls=%fused_computation.12.clone.1 | convolution fusion | flops 12845056 | bytes 2097669 | tf_op jit(solution)/shard_map/while/body/eval_jaxpr/sk,kaf->saf/dot_general | solution.py:82
  100.1 1.8 %convolution_add_fusion.8 = f32[4,128,256]{2,0,1:T(4,128)S(1)} fusion(f32[8,128,256]{2,1,0:T(8,128)S(1)} %fusion.58, f32[4,128,256]{2,0,1:T(4,128)S(1)} %get-tuple-element.410, pred[]{:T(512)S(6)} %compare.7, f32[4,32]{1,0:T(4,128)S(1)} %get-tuple-element.421, s32[]{:T(128)S(6)} %select_n.80), kind=kOutput, calls=%fused_computation.12.clone.1 | convolution fusion | flops 12845056 | bytes 2097669 | tf_op jit(solution)/shard_map/while/body/eval_jaxpr/sk,kaf->saf/dot_general | solution.py:82
  102.9 25.8 %reduce-scatter.5.cloned.1.call-done = f32[128,256]{1,0:T(8,128)} async-done(((f32[512,256]{1,0:T(8,128)}), f32[128,256]{1,0:T(8,128)}) %reduce-scatter.5.cloned.1.call-update) | async-done | bytes 131088 | tf_op jit(solution)/shard_map/reduce_scatter | solution.py:95
  128.7 1.1 fusion.15
  (82 shorter events, 17.1 us)
Async XLA Ops:
  6.5 63.6 %copy-start = (bf16[1,256,256]{2,1,0:T(8,128)(2,1)S(1)}, bf16[1,256,256]{2,1,0:T(8,128)(2,1)}, u32[]{:S(2)}) copy-start(bf16[1,256,256]{2,1,0:T(8,128)(2,1)} %param.18) | copy-start | bytes 393220
  6.5 63.6 %reduce-scatter.3.cloned.1.call-start = ((), (), s32[]{:S(2)}) async-start(), calls=%async_computation.2 | async-start | bytes 655360 | tf_op jit(solution)/shard_map/reduce_scatter | solution.py:91
  8.4 16.3 %copy-start.4 = (bf16[128,256]{1,0:T(8,128)(2,1)}, bf16[128,256]{1,0:T(8,128)(2,1)S(1)}, u32[]{:S(2)}) copy-start(bf16[128,256]{1,0:T(8,128)(2,1)S(1)} %fusion.14) | copy-start | bytes 196612
  42.4 1.0 copy-start.14
  42.5 2.2 %copy-start.1 = (bf16[32,128,128]{2,1,0:T(8,128)(2,1)S(1)}, bf16[32,128,128]{2,1,0:T(8,128)(2,1)}, u32[]{:S(2)}) copy-start(bf16[32,128,128]{2,1,0:T(8,128)(2,1)} %get-tuple-element.431) | copy-start | bytes 3145732
  43.4 1.6 %copy-start.11 = (s32[1,1,32]{2,1,0:T(1,128)S(1)}, s32[1,1,32]{2,1,0:T(1,128)}, u32[]{:S(2)}) copy-start(s32[1,1,32]{2,1,0:T(1,128)} %param.21) | copy-start | bytes 388
  43.4 11.8 %copy-start.5 = (bf16[128,256]{1,0:T(8,128)(2,1)S(1)}, bf16[128,256]{1,0:T(8,128)(2,1)}, u32[]{:S(2)}) copy-start(bf16[128,256]{1,0:T(8,128)(2,1)} %copy-done.4) | copy-start | bytes 196612
  43.4 11.8 %copy-start.6 = (bf16[1,256,256]{2,1,0:T(8,128)(2,1)S(1)}, bf16[1,256,256]{2,1,0:T(8,128)(2,1)}, u32[]{:S(2)}) copy-start(bf16[1,256,256]{2,1,0:T(8,128)(2,1)} %param.17) | copy-start | bytes 393220
  43.4 85.3 %reduce-scatter.5.cloned.1.call-start = ((), (), s32[]{:S(2)}) async-start(), calls=%async_computation.3 | async-start | bytes 655360 | tf_op jit(solution)/shard_map/reduce_scatter | solution.py:95
  43.4 28.2 %copy-start.10 = (f32[256]{0:T(256)S(1)}, f32[256]{0:T(256)}, u32[]{:S(2)}) copy-start(f32[256]{0:T(256)} %param.19) | copy-start | bytes 3076
  55.2 16.6 %copy-start.12 = (f32[128]{0:T(128)}, f32[128]{0:T(128)S(1)}, u32[]{:S(2)}) copy-start(f32[128]{0:T(128)S(1)} %dynamic-slice_rsqrt_fusion) | copy-start | bytes 1540
  71.4 16.6 %copy-start.2 = (f32[128,256]{1,0:T(8,128)}, f32[128,256]{1,0:T(8,128)S(1)}, u32[]{:S(2)}) copy-start(f32[128,256]{1,0:T(8,128)S(1)} %get-tuple-element.292) | copy-start | bytes 393220
  71.7 2.2 %collective-permute-start = (bf16[128,256]{1,0:T(8,128)(2,1)S(1)}, bf16[128,256]{1,0:T(8,128)(2,1)S(1)}, u32[]{:S(2)}, u32[]{:S(2)}) collective-permute-start(bf16[128,256]{1,0:T(8,128)(2,1)S(1)} %fusion.21), channel_id=1, source_target_pairs={{0,16},{1,17},{2,18},{3,19},{4,20},{5,21},{6,22},{7,23},{8,24},{9,... | collective-permute-start | bytes 196616 | tf_op jit(solution)/shard_map/ppermute | solution.py:10
  74.0 14.0 %copy-start.8 = (bf16[128,256]{1,0:T(8,128)(2,1)}, bf16[128,256]{1,0:T(8,128)(2,1)S(1)}, u32[]{:S(2)}) copy-start(bf16[128,256]{1,0:T(8,128)(2,1)S(1)} %collective-permute-done) | copy-start | bytes 196612
  101.9 26.8 %copy-start.13 = (f32[128]{0:T(128)S(1)}, f32[128]{0:T(128)}, u32[]{:S(2)}) copy-start(f32[128]{0:T(128)} %copy-done.12) | copy-start | bytes 1540
  101.9 27.9 %copy-start.7 = (bf16[1,256,256]{2,1,0:T(8,128)(2,1)S(1)}, bf16[1,256,256]{2,1,0:T(8,128)(2,1)}, u32[]{:S(2)}) copy-start(bf16[1,256,256]{2,1,0:T(8,128)(2,1)} %param.17) | copy-start | bytes 393220
  101.9 27.9 %copy-start.9 = (bf16[128,256]{1,0:T(8,128)(2,1)S(1)}, bf16[128,256]{1,0:T(8,128)(2,1)}, u32[]{:S(2)}) copy-start(bf16[128,256]{1,0:T(8,128)(2,1)} %copy-done.8) | copy-start | bytes 196612
  101.9 28.3 %copy-start.3 = (f32[128,256]{1,0:T(8,128)S(1)}, f32[128,256]{1,0:T(8,128)}, u32[]{:S(2)}) copy-start(f32[128,256]{1,0:T(8,128)} %copy-done.2) | copy-start | bytes 393220
Sparse Core Ops, SparseCore 0:
  43.5 26.6 reduce-scatter.2
  103.0 25.6 reduce-scatter.4
where the time goes:
time: 138 us
  waiting for transfers between devices  41.6 us (30%)
  blocking collectives  39.6 us (29%)
  matrix products  24.8 us (18%)
  between operations  14.9 us (11%)
  other arithmetic  8.2 us (6%)
  local copies, waits for them, and re-layouts  7.15 us (5%)
  starting transfers between devices  1.4 us (1%)
    reduce_scatter x2, waiting for transfers between devices, body(): lax.psum_scatter(partial_value, 'rep', scatter_dimension=0, tiled=True)  40.7 us
    all_gather x2, blocking collectives, body(): gathered = lax.all_gather(current, 'row', axis=0, tiled=True)  29.7 us
    dot_general x8, matrix products, add_tiles(): jnp.einsum('sk,kaf->saf', onto_rows, products, precision=lax.Precision.HI...  14.8 us
    unnamed x1, blocking collectives  9.94 us
    dot_general x8, matrix products, add_tiles(): jnp.einsum('kab,kbf->kaf', tile_batch, sources, preferred_element_type=jn...  6.1 us
    select_n x8, other arithmetic, add_tiles(): sources = panel_rows[where_from]  5.87 us
    gather x8, local copies, waits for them, and re-layouts, add_tiles(): sources = panel_rows[where_from]  4.63 us
  transfers between devices with their start and end apart: 3, of which 3 were waited for; matrix products, arithmetic and copies ran while one was open for 1% of the time, Pallas kernels for 0%

commit v1 on v0

--- a/solution.py
+++ b/solution.py
@@ -66,7 +66,14 @@
     )
     current = inputs
     for layer_no in range(2):
-        gathered = lax.all_gather(current, "row", axis=0, tiled=True)
+        ring = [current]
+        for hop in range(3):
+            ring.append(lax.ppermute(ring[-1], "row", [(dev, (dev + 1) % 4) for dev in range(4)]))
+        gathered = jnp.roll(
+            jnp.concatenate(ring[::-1], axis=0),
+            (lax.axis_index("row") + 1) * ring[0].shape[0],
+            axis=0,
+        )
         panel_rows = gathered.reshape(groups, tile_edge, hidden_dim)
         weights_on = placement(all_slots)
 

time: 138 us -> 143 us (1.036)
  blocking collectives: 39.6 us -> 10.2 us
  waiting for transfers between devices: 41.6 us -> 66.9 us
  other arithmetic: 8.2 us -> 12.9 us
  starting transfers between devices: 1.4 us -> 6.03 us
    ppermute x0 -> x6, waiting for transfers between devices: none -> 31.8 us  [body(): lax.ppermute(ring[-1], 'row', [(dev, (dev + 1) % 4) for dev in range(4)])]
    all_gather x2 -> x0, blocking collectives: 29.7 us -> none  [body(): gathered = lax.all_gather(current, 'row', axis=0, tiled=True)]
    reduce_scatter x2, waiting for transfers between devices: 40.7 us -> 34.1 us  [body(): lax.psum_scatter(partial_value, 'rep', scatter_dimension=0, tiled=True)]
    concatenate x0 -> x2, other arithmetic: none -> 4.64 us  [body(): jnp.roll(jnp.concatenate(ring[::-1], axis=0), (lax.axis_index('row') + 1)...]
    ppermute x0 -> x6, starting transfers between devices: none -> 4.62 us  [body(): lax.ppermute(ring[-1], 'row', [(dev, (dev + 1) % 4) for dev in range(4)])]
  transfers between devices with their start and end apart: 3 -> 9, of which waited for: 3 -> 9; matrix products, arithmetic and copies ran while one was open for 1% -> 1% of each run, Pallas kernels for 0% -> 0%
where the time goes in v1:
time: 143 us
  waiting for transfers between devices  66.9 us (47%)
  matrix products  24.8 us (17%)
  between operations  14.9 us (10%)
  other arithmetic  12.9 us (9%)
  blocking collectives  10.2 us (7%)
  local copies, waits for them, and re-layouts  7.13 us (5%)
  starting transfers between devices  6.03 us (4%)
    reduce_scatter x2, waiting for transfers between devices, body(): lax.psum_scatter(partial_value, 'rep', scatter_dimension=0, tiled=True)  34.1 us
    ppermute x6, waiting for transfers between devices, body(): lax.ppermute(ring[-1], 'row', [(dev, (dev + 1) % 4) for dev in range(4)])  31.8 us
    dot_general x8, matrix products, add_tiles(): jnp.einsum('sk,kaf->saf', onto_rows, products, precision=lax.Precision.HI...  14.7 us
    unnamed x1, blocking collectives  10.2 us
    dot_general x8, matrix products, add_tiles(): jnp.einsum('kab,kbf->kaf', tile_batch, sources, preferred_element_type=jn...  6.09 us
    select_n x8, other arithmetic, add_tiles(): sources = panel_rows[where_from]  5.87 us
    concatenate x2, other arithmetic, body(): jnp.roll(jnp.concatenate(ring[::-1], axis=0), (lax.axis_index('row') + 1)...  4.64 us
    gather x8, local copies, waits for them, and re-layouts, add_tiles(): sources = panel_rows[where_from]  4.63 us
  transfers between devices with their start and end apart: 9, of which 9 were waited for; matrix products, arithmetic and copies ran while one was open for 1% of the time, Pallas kernels for 0%

profile of v1, /device:TPU:0, one launch (start us, length us, event | category | flops | bytes accessed | tf_op | source)
XLA Modules:
  0.0 143.0 jit_solution(16432419306355666509)
XLA Ops:
  7.7 3.1 %collective-permute-start = (bf16[128,256]{1,0:T(8,128)(2,1)S(1)}, bf16[128,256]{1,0:T(8,128)(2,1)S(1)}, u32[]{:S(2)}, u32[]{:S(2)}) collective-permute-start(bf16[128,256]{1,0:T(8,128)(2,1)S(1)} %fusion.14), channel_id=1, source_target_pairs={{0,4},{4,8},{8,12},{12,0},{1,5},{5,9},{9,13},{13,1},{2,6},{6,10},{... | collective-permute-start | bytes 196616 | tf_op jit(solution)/shard_map/ppermute | solution.py:71
  11.5 3.6 %collective-permute-done = bf16[128,256]{1,0:T(8,128)(2,1)S(1)} collective-permute-done((bf16[128,256]{1,0:T(8,128)(2,1)S(1)}, bf16[128,256]{1,0:T(8,128)(2,1)S(1)}, u32[]{:S(2)}, u32[]{:S(2)}) %collective-permute-start) | collective-permute-done | bytes 65568 | tf_op jit(solution)/shard_map/ppermute | solution.py:71
  15.1 6.1 %collective-permute-done.1 = bf16[128,256]{1,0:T(8,128)(2,1)S(1)} collective-permute-done((bf16[128,256]{1,0:T(8,128)(2,1)S(1)}, bf16[128,256]{1,0:T(8,128)(2,1)S(1)}, u32[]{:S(2)}, u32[]{:S(2)}) %collective-permute-start.1) | collective-permute-done | bytes 65568 | tf_op jit(solution)/shard_map/ppermute | solution.py:71
  21.8 5.4 %collective-permute-done.2 = bf16[128,256]{1,0:T(8,128)(2,1)S(1)} collective-permute-done((bf16[128,256]{1,0:T(8,128)(2,1)S(1)}, bf16[128,256]{1,0:T(8,128)(2,1)S(1)}, u32[]{:S(2)}, u32[]{:S(2)}) %collective-permute-start.2) | collective-permute-done | bytes 65568 | tf_op jit(solution)/shard_map/ppermute | solution.py:71
  27.2 2.3 %fusion.25 = bf16[512,256]{1,0:T(8,128)(2,1)S(1)} fusion(s32[]{:T(128)S(6)} %select_n.69, bf16[128,256]{1,0:T(8,128)(2,1)S(1)} %collective-permute-done.2, bf16[128,256]{1,0:T(8,128)(2,1)S(1)} %collective-permute-done.1, bf16[128,256]{1,0:T(8,128)(2,1)S(1)} %collective-permute-done, bf16[128,256]{1,0:T(8,128)(2,1)S(1)} %fusion.14), kind=kLoop, calls=%fused_computation.54 | loop fusion | flops 2097152 | bytes 524292 | tf_op jit(solution)/shard_map/jit(_roll_dynamic)/concatenate | solution.py:72
  29.6 17.7 %while.28 = (s32[]{:T(128)}, f32[4,128,256]{2,0,1:T(4,128)S(1)}, f32[4,32]{1,0:T(4,128)S(1)}, bf16[32,128,128]{2,1,0:T(8,128)(2,1)}, s32[32]{0:T(128)}, /*index=...) while((s32[]{:T(128)}, f32[4,128,256]{2,0,1:T(4,128)S(1)}, ...), condition=%wide.region_1.3_spmd.clone, body=%wide.region_0.2_spmd.clone.sunk | while | flops 79954976 | bytes 4985641 | solution.py:94
  32.1 1.8 %convolution_add_fusion.7 = f32[4,128,256]{2,0,1:T(4,128)S(1)} fusion(f32[8,128,256]{2,1,0:T(8,128)S(1)} %fusion.67, f32[4,128,256]{2,0,1:T(4,128)S(1)} %get-tuple-element.381, pred[]{:T(512)S(6)} %compare.7, f32[4,32]{1,0:T(4,128)S(1)} %get-tuple-element.392, s32[]{:T(128)S(6)} %select_n.94), kind=kOutput, calls=%fused_computation.2.clone.1 | convolution fusion | flops 12845056 | bytes 2097669 | tf_op jit(solution)/shard_map/while/body/eval_jaxpr/sk,kaf->saf/dot_general | solution.py:89
  36.6 1.8 %convolution_add_fusion.7 = f32[4,128,256]{2,0,1:T(4,128)S(1)} fusion(f32[8,128,256]{2,1,0:T(8,128)S(1)} %fusion.67, f32[4,128,256]{2,0,1:T(4,128)S(1)} %get-tuple-element.381, pred[]{:T(512)S(6)} %compare.7, f32[4,32]{1,0:T(4,128)S(1)} %get-tuple-element.392, s32[]{:T(128)S(6)} %select_n.94), kind=kOutput, calls=%fused_computation.2.clone.1 | convolution fusion | flops 12845056 | bytes 2097669 | tf_op jit(solution)/shard_map/while/body/eval_jaxpr/sk,kaf->saf/dot_general | solution.py:89
  41.0 1.8 %convolution_add_fusion.7 = f32[4,128,256]{2,0,1:T(4,128)S(1)} fusion(f32[8,128,256]{2,1,0:T(8,128)S(1)} %fusion.67, f32[4,128,256]{2,0,1:T(4,128)S(1)} %get-tuple-element.381, pred[]{:T(512)S(6)} %compare.7, f32[4,32]{1,0:T(4,128)S(1)} %get-tuple-element.392, s32[]{:T(128)S(6)} %select_n.94), kind=kOutput, calls=%fused_computation.2.clone.1 | convolution fusion | flops 12845056 | bytes 2097669 | tf_op jit(solution)/shard_map/while/body/eval_jaxpr/sk,kaf->saf/dot_general | solution.py:89
  45.5 1.8 %convolution_add_fusion.7 = f32[4,128,256]{2,0,1:T(4,128)S(1)} fusion(f32[8,128,256]{2,1,0:T(8,128)S(1)} %fusion.67, f32[4,128,256]{2,0,1:T(4,128)S(1)} %get-tuple-element.381, pred[]{:T(512)S(6)} %compare.7, f32[4,32]{1,0:T(4,128)S(1)} %get-tuple-element.392, s32[]{:T(128)S(6)} %select_n.94), kind=kOutput, calls=%fused_computation.2.clone.1 | convolution fusion | flops 12845056 | bytes 2097669 | tf_op jit(solution)/shard_map/while/body/eval_jaxpr/sk,kaf->saf/dot_general | solution.py:89
  49.9 10.2 %all-reduce = f32[512]{0:T(512)S(1)} all-reduce(f32[512]{0:T(512)S(1)} %convolution_bitcast_fusion), channel_id=3, replica_groups=mesh['layer'=2,'row'=4,'rep'=4] {'rep'}, use_global_device_ids=true, to_apply=%region_4.6.clone | all-reduce | flops 512 | bytes 4096
  60.4 11.6 %reduce-scatter.3.cloned.1.call-done = f32[128,256]{1,0:T(8,128)} async-done(((f32[512,256]{1,0:T(8,128)}), f32[128,256]{1,0:T(8,128)}) %reduce-scatter.3.cloned.1.call-update) | async-done | bytes 131088 | tf_op jit(solution)/shard_map/reduce_scatter | solution.py:98
  73.5 1.4 collective-permute-start.3
  75.8 1.5 %collective-permute-start.4 = (bf16[128,256]{1,0:T(8,128)(2,1)S(1)}, bf16[128,256]{1,0:T(8,128)(2,1)S(1)}, u32[]{:S(2)}, u32[]{:S(2)}) collective-permute-start(bf16[128,256]{1,0:T(8,128)(2,1)S(1)} %collective-permute-done.3), channel_id=1, source_target_pairs={{0,4},{4,8},{8,12},{12,0},{1,5},{5,9},{9,13},{13,1},{2,6},{6,10},{... | collective-permute-start | bytes 196616 | tf_op jit(solution)/shard_map/ppermute | solution.py:71
  77.3 4.6 %collective-permute-done.4 = bf16[128,256]{1,0:T(8,128)(2,1)S(1)} collective-permute-done((bf16[128,256]{1,0:T(8,128)(2,1)S(1)}, bf16[128,256]{1,0:T(8,128)(2,1)S(1)}, u32[]{:S(2)}, u32[]{:S(2)}) %collective-permute-start.4) | collective-permute-done | bytes 65568 | tf_op jit(solution)/shard_map/ppermute | solution.py:71
  81.9 6.1 %collective-permute-done.5 = bf16[128,256]{1,0:T(8,128)(2,1)S(1)} collective-permute-done((bf16[128,256]{1,0:T(8,128)(2,1)S(1)}, bf16[128,256]{1,0:T(8,128)(2,1)S(1)}, u32[]{:S(2)}, u32[]{:S(2)}) %collective-permute-start.5) | collective-permute-done | bytes 65568 | tf_op jit(solution)/shard_map/ppermute | solution.py:71
  88.0 6.1 %collective-permute-done.6 = bf16[128,256]{1,0:T(8,128)(2,1)S(1)} collective-permute-done((bf16[128,256]{1,0:T(8,128)(2,1)S(1)}, bf16[128,256]{1,0:T(8,128)(2,1)S(1)}, u32[]{:S(2)}, u32[]{:S(2)}) %collective-permute-start.6) | collective-permute-done | bytes 65568 | tf_op jit(solution)/shard_map/ppermute | solution.py:71
  94.1 2.3 %fusion.18 = bf16[512,256]{1,0:T(8,128)(2,1)S(1)} fusion(s32[]{:T(128)S(6)} %select_n.69, bf16[128,256]{1,0:T(8,128)(2,1)S(1)} %collective-permute-done.6, bf16[128,256]{1,0:T(8,128)(2,1)S(1)} %collective-permute-done.5, bf16[128,256]{1,0:T(8,128)(2,1)S(1)} %collective-permute-done.4, bf16[128,256]{1,0:T(8,128)(2,1)S(1)} %collective-permute-done.3), kind=kLoop, calls=%fused_computation.47 | loop fusion | flops 2097152 | bytes 524292 | tf_op jit(solution)/shard_map/jit(_roll_dynamic)/concatenate | solution.py:72
  96.4 13.9 %while.29 = (s32[]{:T(128)}, f32[4,128,256]{2,0,1:T(4,128)S(1)}, f32[4,32]{1,0:T(4,128)S(1)}, bf16[32,128,128]{2,1,0:T(8,128)(2,1)S(1)}, s32[32]{0:T(128)}, /*in...) while((s32[]{:T(128)}, f32[4,128,256]{2,0,1:T(4,128)S(1)}, ...), condition=%wide.region_8.10_spmd.clone, body=%wide.region_7.9_spmd.clone.sunk | while | flops 79954976 | bytes 4985641 | solution.py:94
  98.1 1.8 %convolution_add_fusion.8 = f32[4,128,256]{2,0,1:T(4,128)S(1)} fusion(f32[8,128,256]{2,1,0:T(8,128)S(1)} %fusion.72, f32[4,128,256]{2,0,1:T(4,128)S(1)} %get-tuple-element.411, pred[]{:T(512)S(6)} %compare.8, f32[4,32]{1,0:T(4,128)S(1)} %get-tuple-element.422, s32[]{:T(128)S(6)} %select_n.96), kind=kOutput, calls=%fused_computation.12.clone.1 | convolution fusion | flops 12845056 | bytes 2097669 | tf_op jit(solution)/shard_map/while/body/eval_jaxpr/sk,kaf->saf/dot_general | solution.py:89
  101.5 1.8 %convolution_add_fusion.8 = f32[4,128,256]{2,0,1:T(4,128)S(1)} fusion(f32[8,128,256]{2,1,0:T(8,128)S(1)} %fusion.72, f32[4,128,256]{2,0,1:T(4,128)S(1)} %get-tuple-element.411, pred[]{:T(512)S(6)} %compare.8, f32[4,32]{1,0:T(4,128)S(1)} %get-tuple-element.422, s32[]{:T(128)S(6)} %select_n.96), kind=kOutput, calls=%fused_computation.12.clone.1 | convolution fusion | flops 12845056 | bytes 2097669 | tf_op jit(solution)/shard_map/while/body/eval_jaxpr/sk,kaf->saf/dot_general | solution.py:89
  105.0 1.8 %convolution_add_fusion.8 = f32[4,128,256]{2,0,1:T(4,128)S(1)} fusion(f32[8,128,256]{2,1,0:T(8,128)S(1)} %fusion.72, f32[4,128,256]{2,0,1:T(4,128)S(1)} %get-tuple-element.411, pred[]{:T(512)S(6)} %compare.8, f32[4,32]{1,0:T(4,128)S(1)} %get-tuple-element.422, s32[]{:T(128)S(6)} %select_n.96), kind=kOutput, calls=%fused_computation.12.clone.1 | convolution fusion | flops 12845056 | bytes 2097669 | tf_op jit(solution)/shard_map/while/body/eval_jaxpr/sk,kaf->saf/dot_general | solution.py:89
  108.5 1.8 %convolution_add_fusion.8 = f32[4,128,256]{2,0,1:T(4,128)S(1)} fusion(f32[8,128,256]{2,1,0:T(8,128)S(1)} %fusion.72, f32[4,128,256]{2,0,1:T(4,128)S(1)} %get-tuple-element.411, pred[]{:T(512)S(6)} %compare.8, f32[4,32]{1,0:T(4,128)S(1)} %get-tuple-element.422, s32[]{:T(128)S(6)} %select_n.96), kind=kOutput, calls=%fused_computation.12.clone.1 | convolution fusion | flops 12845056 | bytes 2097669 | tf_op jit(solution)/shard_map/while/body/eval_jaxpr/sk,kaf->saf/dot_general | solution.py:89
  111.3 22.5 %reduce-scatter.5.cloned.1.call-done = f32[128,256]{1,0:T(8,128)} async-done(((f32[512,256]{1,0:T(8,128)}), f32[128,256]{1,0:T(8,128)}) %reduce-scatter.5.cloned.1.call-update) | async-done | bytes 131088 | tf_op jit(solution)/shard_map/reduce_scatter | solution.py:102
  (94 shorter events, 26.4 us)
Async XLA Ops:
  6.5 65.5 %copy-start = (bf16[1,256,256]{2,1,0:T(8,128)(2,1)S(1)}, bf16[1,256,256]{2,1,0:T(8,128)(2,1)}, u32[]{:S(2)}) copy-start(bf16[1,256,256]{2,1,0:T(8,128)(2,1)} %param.20) | copy-start | bytes 393220
  6.5 65.5 %reduce-scatter.3.cloned.1.call-start = ((), (), s32[]{:S(2)}) async-start(), calls=%async_computation.2 | async-start | bytes 655360 | tf_op jit(solution)/shard_map/reduce_scatter | solution.py:98
  7.7 21.8 %copy-start.4 = (bf16[128,256]{1,0:T(8,128)(2,1)}, bf16[128,256]{1,0:T(8,128)(2,1)S(1)}, u32[]{:S(2)}) copy-start(bf16[128,256]{1,0:T(8,128)(2,1)S(1)} %fusion.14) | copy-start | bytes 196612
  7.7 7.4 %collective-permute-start = (bf16[128,256]{1,0:T(8,128)(2,1)S(1)}, bf16[128,256]{1,0:T(8,128)(2,1)S(1)}, u32[]{:S(2)}, u32[]{:S(2)}) collective-permute-start(bf16[128,256]{1,0:T(8,128)(2,1)S(1)} %fusion.14), channel_id=1, source_target_pairs={{0,4},{4,8},{8,12},{12,0},{1,5},{5,9},{9,13},{13,1},{2,6},{6,10},{... | collective-permute-start | bytes 196616 | tf_op jit(solution)/shard_map/ppermute | solution.py:71
  15.1 6.1 %collective-permute-start.1 = (bf16[128,256]{1,0:T(8,128)(2,1)S(1)}, bf16[128,256]{1,0:T(8,128)(2,1)S(1)}, u32[]{:S(2)}, u32[]{:S(2)}) collective-permute-start(bf16[128,256]{1,0:T(8,128)(2,1)S(1)} %collective-permute-done), channel_id=1, source_target_pairs={{0,4},{4,8},{8,12},{12,0},{1,5},{5,9},{9,13},{13,1},{2,6},{6,10},{... | collective-permute-start | bytes 196616 | tf_op jit(solution)/shard_map/ppermute | solution.py:71
  21.2 6.1 %collective-permute-start.2 = (bf16[128,256]{1,0:T(8,128)(2,1)S(1)}, bf16[128,256]{1,0:T(8,128)(2,1)S(1)}, u32[]{:S(2)}, u32[]{:S(2)}) collective-permute-start(bf16[128,256]{1,0:T(8,128)(2,1)S(1)} %collective-permute-done.1), channel_id=1, source_target_pairs={{0,4},{4,8},{8,12},{12,0},{1,5},{5,9},{9,13},{13,1},{2,6},{6,10},{... | collective-permute-start | bytes 196616 | tf_op jit(solution)/shard_map/ppermute | solution.py:71
  47.3 1.0 copy-start.14
  47.3 2.1 %copy-start.1 = (bf16[32,128,128]{2,1,0:T(8,128)(2,1)S(1)}, bf16[32,128,128]{2,1,0:T(8,128)(2,1)}, u32[]{:S(2)}) copy-start(bf16[32,128,128]{2,1,0:T(8,128)(2,1)} %get-tuple-element.432) | copy-start | bytes 3145732
  48.2 1.6 %copy-start.11 = (s32[1,1,32]{2,1,0:T(1,128)S(1)}, s32[1,1,32]{2,1,0:T(1,128)}, u32[]{:S(2)}) copy-start(s32[1,1,32]{2,1,0:T(1,128)} %param.23) | copy-start | bytes 388
  48.2 12.0 %copy-start.5 = (bf16[128,256]{1,0:T(8,128)(2,1)S(1)}, bf16[128,256]{1,0:T(8,128)(2,1)}, u32[]{:S(2)}) copy-start(bf16[128,256]{1,0:T(8,128)(2,1)} %copy-done.4) | copy-start | bytes 196612
  48.2 12.0 %copy-start.6 = (bf16[1,256,256]{2,1,0:T(8,128)(2,1)S(1)}, bf16[1,256,256]{2,1,0:T(8,128)(2,1)}, u32[]{:S(2)}) copy-start(bf16[1,256,256]{2,1,0:T(8,128)(2,1)} %param.19) | copy-start | bytes 393220
  48.3 85.6 %reduce-scatter.5.cloned.1.call-start = ((), (), s32[]{:S(2)}) async-start(), calls=%async_computation.3 | async-start | bytes 655360 | tf_op jit(solution)/shard_map/reduce_scatter | solution.py:102
  48.3 25.1 %copy-start.10 = (f32[256]{0:T(256)S(1)}, f32[256]{0:T(256)}, u32[]{:S(2)}) copy-start(f32[256]{0:T(256)} %param.21) | copy-start | bytes 3076
  60.2 21.7 %copy-start.12 = (f32[128]{0:T(128)}, f32[128]{0:T(128)S(1)}, u32[]{:S(2)}) copy-start(f32[128]{0:T(128)S(1)} %dynamic-slice_rsqrt_fusion) | copy-start | bytes 1540
  73.2 23.2 %copy-start.2 = (f32[128,256]{1,0:T(8,128)}, f32[128,256]{1,0:T(8,128)S(1)}, u32[]{:S(2)}) copy-start(f32[128,256]{1,0:T(8,128)S(1)} %get-tuple-element.293) | copy-start | bytes 393220
  73.5 2.3 %collective-permute-start.3 = (bf16[128,256]{1,0:T(8,128)(2,1)S(1)}, bf16[128,256]{1,0:T(8,128)(2,1)S(1)}, u32[]{:S(2)}, u32[]{:S(2)}) collective-permute-start(bf16[128,256]{1,0:T(8,128)(2,1)S(1)} %fusion.35), channel_id=1, source_target_pairs={{0,16},{1,17},{2,18},{3,19},{4,20},{5,21},{6,22},{7,23},{8,24},{9,... | collective-permute-start | bytes 196616 | tf_op jit(solution)/shard_map/ppermute | solution.py:10
  75.8 20.6 %copy-start.8 = (bf16[128,256]{1,0:T(8,128)(2,1)}, bf16[128,256]{1,0:T(8,128)(2,1)S(1)}, u32[]{:S(2)}) copy-start(bf16[128,256]{1,0:T(8,128)(2,1)S(1)} %collective-permute-done.3) | copy-start | bytes 196612
  75.8 6.1 %collective-permute-start.4 = (bf16[128,256]{1,0:T(8,128)(2,1)S(1)}, bf16[128,256]{1,0:T(8,128)(2,1)S(1)}, u32[]{:S(2)}, u32[]{:S(2)}) collective-permute-start(bf16[128,256]{1,0:T(8,128)(2,1)S(1)} %collective-permute-done.3), channel_id=1, source_target_pairs={{0,4},{4,8},{8,12},{12,0},{1,5},{5,9},{9,13},{13,1},{2,6},{6,10},{... | collective-permute-start | bytes 196616 | tf_op jit(solution)/shard_map/ppermute | solution.py:71
  81.9 6.1 %collective-permute-start.5 = (bf16[128,256]{1,0:T(8,128)(2,1)S(1)}, bf16[128,256]{1,0:T(8,128)(2,1)S(1)}, u32[]{:S(2)}, u32[]{:S(2)}) collective-permute-start(bf16[128,256]{1,0:T(8,128)(2,1)S(1)} %collective-permute-done.4), channel_id=1, source_target_pairs={{0,4},{4,8},{8,12},{12,0},{1,5},{5,9},{9,13},{13,1},{2,6},{6,10},{... | collective-permute-start | bytes 196616 | tf_op jit(solution)/shard_map/ppermute | solution.py:71
  88.0 6.1 %collective-permute-start.6 = (bf16[128,256]{1,0:T(8,128)(2,1)S(1)}, bf16[128,256]{1,0:T(8,128)(2,1)S(1)}, u32[]{:S(2)}, u32[]{:S(2)}) collective-permute-start(bf16[128,256]{1,0:T(8,128)(2,1)S(1)} %collective-permute-done.5), channel_id=1, source_target_pairs={{0,4},{4,8},{8,12},{12,0},{1,5},{5,9},{9,13},{13,1},{2,6},{6,10},{... | collective-permute-start | bytes 196616 | tf_op jit(solution)/shard_map/ppermute | solution.py:71
  110.3 23.5 %copy-start.13 = (f32[128]{0:T(128)S(1)}, f32[128]{0:T(128)}, u32[]{:S(2)}) copy-start(f32[128]{0:T(128)} %copy-done.12) | copy-start | bytes 1540
  110.3 24.6 %copy-start.7 = (bf16[1,256,256]{2,1,0:T(8,128)(2,1)S(1)}, bf16[1,256,256]{2,1,0:T(8,128)(2,1)}, u32[]{:S(2)}) copy-start(bf16[1,256,256]{2,1,0:T(8,128)(2,1)} %param.19) | copy-start | bytes 393220
  110.3 24.6 %copy-start.9 = (bf16[128,256]{1,0:T(8,128)(2,1)S(1)}, bf16[128,256]{1,0:T(8,128)(2,1)}, u32[]{:S(2)}) copy-start(bf16[128,256]{1,0:T(8,128)(2,1)} %copy-done.8) | copy-start | bytes 196612
  110.4 25.0 %copy-start.3 = (f32[128,256]{1,0:T(8,128)S(1)}, f32[128,256]{1,0:T(8,128)}, u32[]{:S(2)}) copy-start(f32[128,256]{1,0:T(8,128)} %copy-done.2) | copy-start | bytes 393220
Sparse Core Ops, SparseCore 0:
  48.4 23.5 reduce-scatter.2
  111.4 22.3 reduce-scatter.4
